TPU v7x, 32 devices: a whole 2x2x4 slice. The times are simulated.
32 devices in a mesh: dp: 8 (over z, y), tensor: 4 (over x, core).
Axes of the slice: x: 2, y: 2, z: 4, core: 2. Of those that a mesh axis runs over, the one named last changes fastest.
Arguments:
- hidden: bfloat16 [8, 832, 1024], P('dp'), may hold values from -6 to 6
- text_states: bfloat16 [8, 256, 1024], P('dp'), may hold values from -6 to 6
- text_len: int32 [8], P('dp'), may hold values from 1 to 256, as said below
- ln1_gain: float32 [1024], replicated, may hold values from 0.5 to 1.5
- ln1_bias: float32 [1024], replicated, may hold values from -3 to 3
- self_q: bfloat16 [1024, 1024], P(None, 'tensor'), may hold values from -0.1875 to 0.1875
- self_k: bfloat16 [1024, 1024], P(None, 'tensor'), may hold values from -0.1875 to 0.1875
- self_v: bfloat16 [1024, 1024], P(None, 'tensor'), may hold values from -0.1875 to 0.1875
- self_o: bfloat16 [1024, 1024], P('tensor'), may hold values from -1.5 to 1.5
- ln2_gain: float32 [1024], replicated, may hold values from 0.5 to 1.5
- ln2_bias: float32 [1024], replicated, may hold values from -3 to 3
- cross_q: bfloat16 [1024, 1024], P(None, 'tensor'), may hold values from -0.1875 to 0.1875
- cross_k: bfloat16 [1024, 1024], P(None, 'tensor'), may hold values from -0.1875 to 0.1875
- cross_v: bfloat16 [1024, 1024], P(None, 'tensor'), may hold values from -0.1875 to 0.1875
- cross_o: bfloat16 [1024, 1024], P('tensor'), may hold values from -0.75 to 0.75
- ln3_gain: float32 [1024], replicated, may hold values from 0.5 to 1.5
- ln3_bias: float32 [1024], replicated, may hold values from -3 to 3
- ffn_up: bfloat16 [1024, 4096], P(None, 'tensor'), may hold values from -0.1875 to 0.1875
- ffn_down: bfloat16 [4096, 1024], P('tensor'), may hold values from -0.09375 to 0.09375
- cotangent: bfloat16 [8, 832, 1024], P('dp'), may hold values from -6 to 6
Outputs:
- output: bfloat16 [8, 832, 1024], P('dp')
- hidden_grad: bfloat16 [8, 832, 1024], P('dp')
- text_grad: float32 [8, 256, 1024], P('dp')
- ln1_gain_grad: float32 [1024], P('dp')
- ln1_bias_grad: float32 [1024], P('dp')
- self_q_grad: float32 [1024, 1024], P('dp', 'tensor')
- self_k_grad: float32 [1024, 1024], P('dp', 'tensor')
- self_v_grad: float32 [1024, 1024], P('dp', 'tensor')
- self_o_grad: float32 [1024, 1024], P('tensor', 'dp')
- ln2_gain_grad: float32 [1024], P('dp')
- ln2_bias_grad: float32 [1024], P('dp')
- cross_q_grad: float32 [1024, 1024], P('dp', 'tensor')
- cross_k_grad: float32 [1024, 1024], P('dp', 'tensor')
- cross_v_grad: float32 [1024, 1024], P('dp', 'tensor')
- cross_o_grad: float32 [1024, 1024], P('tensor', 'dp')
- ln3_gain_grad: float32 [1024], P('dp')
- ln3_bias_grad: float32 [1024], P('dp')
- ffn_up_grad: float32 [1024, 4096], P('dp', 'tensor')
- ffn_down_grad: float32 [4096, 1024], P('tensor', 'dp')
Inputs may be any that keep to these rules, and one draw needn't show every extreme that they name: Clip c attends to text slots below text_len[c]; the other slots of its 256 are padding. Some clip uses all 256.
All inputs are finite; a program needn't handle non-finite values.
Results may differ from a plain program's by a relative error of at most 0.019.
Values sent between devices are 32-bit elements; how exact they have to be, the bound alone decides.
No kernel may reach another device: no remote copies, remote signals or barrier semaphores. Data moves between devices by JAX's collectives and lax.ppermute only.
A program may use at most 192 MiB of HBM per device.

v0:
```python
import jax
import jax.numpy as jnp
from jax import lax
from jax.sharding import PartitionSpec as P

HD = 64


EPS = 1e-05
NEG = -1e30


def norm_forward(values, gain_vec, shift_vec):
    row_mean = jnp.mean(values, -1, keepdims=True)
    centred = values - row_mean
    variance = jnp.mean(centred * centred, -1, keepdims=True)
    inverse = lax.rsqrt(variance + EPS)
    scaled = centred * inverse
    return (scaled * gain_vec + shift_vec, scaled, inverse)


def norm_backward(grad_out, scaled, inverse, gain_vec):
    weighted = grad_out * gain_vec
    first_mean = jnp.mean(weighted, -1, keepdims=True)
    second_mean = jnp.mean(weighted * scaled, -1, keepdims=True)
    grad_in = inverse * (weighted - first_mean - scaled * second_mean)
    return (grad_in, jnp.sum(grad_out * scaled, 0), jnp.sum(grad_out, 0))


def over_rows(left_op, right_op):
    return lax.dot_general(
        left_op, right_op, (((0,), (0,)), ((), ())), preferred_element_type=jnp.float32
    )


def against(left_op, right_op):
    return lax.dot_general(
        left_op, right_op, (((1,), (1,)), ((), ())), preferred_element_type=jnp.float32
    )


def project(row_block, weight):
    return jnp.dot(row_block, weight, preferred_element_type=jnp.float32).astype(jnp.bfloat16)


def split_heads(values, clip_count):
    return values.reshape(clip_count, -1, values.shape[-1] // HD, HD)


def masked_scores(query_heads, key_heads, allowed):
    scores = jnp.einsum(
        "cqhd,ckhd->chqk", query_heads, key_heads, preferred_element_type=jnp.float32
    ) * HD ** (-0.5)
    return jnp.where(allowed[:, None], scores, NEG)


def attend_forward(query_heads, key_heads, value_heads, allowed):
    scores = masked_scores(query_heads, key_heads, allowed)
    row_top = jnp.max(scores, -1, keepdims=True)
    exp_total = jnp.sum(jnp.exp(scores - row_top), -1, keepdims=True)
    log_total = row_top + jnp.log(exp_total)
    probs_low = jnp.exp(scores - log_total).astype(jnp.bfloat16)
    mixed_out = jnp.einsum(
        "chqk,ckhd->cqhd", probs_low, value_heads, preferred_element_type=jnp.float32
    )
    return (mixed_out.astype(jnp.bfloat16), log_total)


def attend_backward(query_heads, key_heads, value_heads, allowed, log_total, mixed_grad):
    scores = masked_scores(query_heads, key_heads, allowed)
    prob_f32 = jnp.exp(scores - log_total)
    value_grad = jnp.einsum(
        "chqk,cqhd->ckhd",
        prob_f32.astype(jnp.bfloat16),
        mixed_grad,
        preferred_element_type=jnp.float32,
    )
    prob_grad = jnp.einsum(
        "cqhd,ckhd->chqk", mixed_grad, value_heads, preferred_element_type=jnp.float32
    )
    score_grad = prob_f32 * (prob_grad - jnp.sum(prob_f32 * prob_grad, -1, keepdims=True))
    score_low = score_grad.astype(jnp.bfloat16)
    query_grad = jnp.einsum(
        "chqk,ckhd->cqhd", score_low, key_heads, preferred_element_type=jnp.float32
    ) * HD ** (-0.5)
    key_grad = jnp.einsum(
        "chqk,cqhd->ckhd", score_low, query_heads, preferred_element_type=jnp.float32
    ) * HD ** (-0.5)
    return (
        query_grad.astype(jnp.bfloat16),
        key_grad.astype(jnp.bfloat16),
        value_grad.astype(jnp.bfloat16),
    )


def gelu_exact(values):
    return jax.nn.gelu(values, approximate=False)


def body(
    hidden,
    text_states,
    text_len,
    ln1_gain,
    ln1_bias,
    self_q,
    self_k,
    self_v,
    self_o,
    ln2_gain,
    ln2_bias,
    cross_q,
    cross_k,
    cross_v,
    cross_o,
    ln3_gain,
    ln3_bias,
    ffn_up,
    ffn_down,
    cotangent,
):
    clip_count, frames, model_width = hidden.shape
    text_rows = text_states.shape[1]
    row_count = clip_count * frames
    position = jnp.arange(frames)
    causal = jnp.broadcast_to(position[:, None] >= position[None, :], (clip_count, frames, frames))
    text_mask = jnp.broadcast_to(
        jnp.arange(text_rows)[None, None, :] < text_len[:, None, None],
        (clip_count, frames, text_rows),
    )
    resid_in = hidden.astype(jnp.float32).reshape(row_count, model_width)
    norm_one, scaled_one, inverse_one = norm_forward(resid_in, ln1_gain, ln1_bias)
    norm_one_low = norm_one.astype(jnp.bfloat16)
    query_one = split_heads(project(norm_one_low, self_q), clip_count)
    key_one = split_heads(project(norm_one_low, self_k), clip_count)
    value_one = split_heads(project(norm_one_low, self_v), clip_count)
    mixed_one, total_one = attend_forward(query_one, key_one, value_one, causal)
    mixed_one_rows = mixed_one.reshape(row_count, -1)
    first_sum = resid_in + lax.psum(
        jnp.dot(mixed_one_rows, self_o, preferred_element_type=jnp.float32), "tensor"
    )
    norm_two, scaled_two, inverse_two = norm_forward(first_sum, ln2_gain, ln2_bias)
    norm_two_low = norm_two.astype(jnp.bfloat16)
    text_flat = text_states.reshape(clip_count * text_rows, model_width)
    query_two = split_heads(project(norm_two_low, cross_q), clip_count)
    key_two = split_heads(project(text_flat, cross_k), clip_count)
    value_two = split_heads(project(text_flat, cross_v), clip_count)
    mixed_two, total_two = attend_forward(query_two, key_two, value_two, text_mask)
    mixed_two_rows = mixed_two.reshape(row_count, -1)
    second_sum = first_sum + lax.psum(
        jnp.dot(mixed_two_rows, cross_o, preferred_element_type=jnp.float32), "tensor"
    )
    norm_three, scaled_three, inverse_three = norm_forward(second_sum, ln3_gain, ln3_bias)
    norm_three_low = norm_three.astype(jnp.bfloat16)
    inner_pre = jnp.dot(norm_three_low, ffn_up, preferred_element_type=jnp.float32)
    active, gelu_pull = jax.vjp(gelu_exact, inner_pre)
    active_low = active.astype(jnp.bfloat16)
    final_sum = second_sum + lax.psum(
        jnp.dot(active_low, ffn_down, preferred_element_type=jnp.float32), "tensor"
    )
    output = final_sum.astype(jnp.bfloat16).reshape(clip_count, frames, model_width)
    out_grad = cotangent.reshape(row_count, model_width)
    down_grad = over_rows(active_low, out_grad)
    active_grad = against(out_grad, ffn_down).astype(jnp.bfloat16)
    inner_grad = gelu_pull(active_grad.astype(jnp.float32))[0].astype(jnp.bfloat16)
    up_grad = over_rows(norm_three_low, inner_grad)
    norm_three_grad = lax.psum(against(inner_grad, ffn_up), "tensor")
    delta_in, gain3_grad, bias3_grad = norm_backward(
        norm_three_grad, scaled_three, inverse_three, ln3_gain
    )
    grad_resid = out_grad.astype(jnp.float32) + delta_in
    resid_low = grad_resid.astype(jnp.bfloat16)
    co_grad = over_rows(mixed_two_rows, resid_low)
    mixed_two_grad = split_heads(against(resid_low, cross_o).astype(jnp.bfloat16), clip_count)
    query_two_grad, key_two_grad, value_two_grad = attend_backward(
        query_two, key_two, value_two, text_mask, total_two, mixed_two_grad
    )
    query_two_rows = query_two_grad.reshape(row_count, -1)
    key_two_rows = key_two_grad.reshape(clip_count * text_rows, -1)
    value_two_rows = value_two_grad.reshape(clip_count * text_rows, -1)
    cq_grad = over_rows(norm_two_low, query_two_rows)
    ck_grad = over_rows(text_flat, key_two_rows)
    cv_grad = over_rows(text_flat, value_two_rows)
    norm_two_part = against(query_two_rows, cross_q)
    text_part = against(key_two_rows, cross_k) + against(value_two_rows, cross_v)
    norm_two_grad, text_sum = lax.psum((norm_two_part, text_part), "tensor")
    text_grad = text_sum.reshape(clip_count, text_rows, model_width)
    delta_in, gain2_grad, bias2_grad = norm_backward(
        norm_two_grad, scaled_two, inverse_two, ln2_gain
    )
    grad_resid = grad_resid + delta_in
    resid_low = grad_resid.astype(jnp.bfloat16)
    so_grad = over_rows(mixed_one_rows, resid_low)
    mixed_one_grad = split_heads(against(resid_low, self_o).astype(jnp.bfloat16), clip_count)
    query_one_grad, key_one_grad, value_one_grad = attend_backward(
        query_one, key_one, value_one, causal, total_one, mixed_one_grad
    )
    query_one_rows = query_one_grad.reshape(row_count, -1)
    key_one_rows = key_one_grad.reshape(row_count, -1)
    value_one_rows = value_one_grad.reshape(row_count, -1)
    sq_grad = over_rows(norm_one_low, query_one_rows)
    sk_grad = over_rows(norm_one_low, key_one_rows)
    sv_grad = over_rows(norm_one_low, value_one_rows)
    norm_one_part = (
        against(query_one_rows, self_q)
        + against(key_one_rows, self_k)
        + against(value_one_rows, self_v)
    )
    norm_one_grad = lax.psum(norm_one_part, "tensor")
    delta_in, gain1_grad, bias1_grad = norm_backward(
        norm_one_grad, scaled_one, inverse_one, ln1_gain
    )
    hidden_grad = (
        (grad_resid + delta_in).astype(jnp.bfloat16).reshape(clip_count, frames, model_width)
    )
    (
        gain1_grad,
        bias1_grad,
        sq_grad,
        sk_grad,
        sv_grad,
        so_grad,
        gain2_grad,
        bias2_grad,
        cq_grad,
        ck_grad,
        cv_grad,
        co_grad,
        gain3_grad,
        bias3_grad,
        up_grad,
        down_grad,
    ) = (
        lax.psum_scatter(gain1_grad, "dp", scatter_dimension=0, tiled=True),
        lax.psum_scatter(bias1_grad, "dp", scatter_dimension=0, tiled=True),
        lax.psum_scatter(sq_grad, "dp", scatter_dimension=0, tiled=True),
        lax.psum_scatter(sk_grad, "dp", scatter_dimension=0, tiled=True),
        lax.psum_scatter(sv_grad, "dp", scatter_dimension=0, tiled=True),
        lax.psum_scatter(so_grad, "dp", scatter_dimension=1, tiled=True),
        lax.psum_scatter(gain2_grad, "dp", scatter_dimension=0, tiled=True),
        lax.psum_scatter(bias2_grad, "dp", scatter_dimension=0, tiled=True),
        lax.psum_scatter(cq_grad, "dp", scatter_dimension=0, tiled=True),
        lax.psum_scatter(ck_grad, "dp", scatter_dimension=0, tiled=True),
        lax.psum_scatter(cv_grad, "dp", scatter_dimension=0, tiled=True),
        lax.psum_scatter(co_grad, "dp", scatter_dimension=1, tiled=True),
        lax.psum_scatter(gain3_grad, "dp", scatter_dimension=0, tiled=True),
        lax.psum_scatter(bias3_grad, "dp", scatter_dimension=0, tiled=True),
        lax.psum_scatter(up_grad, "dp", scatter_dimension=0, tiled=True),
        lax.psum_scatter(down_grad, "dp", scatter_dimension=1, tiled=True),
    )
    return (
        output,
        hidden_grad,
        text_grad,
        gain1_grad,
        bias1_grad,
        sq_grad,
        sk_grad,
        sv_grad,
        so_grad,
        gain2_grad,
        bias2_grad,
        cq_grad,
        ck_grad,
        cv_grad,
        co_grad,
        gain3_grad,
        bias3_grad,
        up_grad,
        down_grad,
    )


def solution(mesh):
    in_specs = (
        P("dp", None, None),
        P("dp", None, None),
        P("dp"),
        P(),
        P(),
        P(None, "tensor"),
        P(None, "tensor"),
        P(None, "tensor"),
        P("tensor", None),
        P(),
        P(),
        P(None, "tensor"),
        P(None, "tensor"),
        P(None, "tensor"),
        P("tensor", None),
        P(),
        P(),
        P(None, "tensor"),
        P("tensor", None),
        P("dp", None, None),
    )
    out_specs = (
        P("dp", None, None),
        P("dp", None, None),
        P("dp", None, None),
        P("dp"),
        P("dp"),
        P("dp", "tensor"),
        P("dp", "tensor"),
        P("dp", "tensor"),
        P("tensor", "dp"),
        P("dp"),
        P("dp"),
        P("dp", "tensor"),
        P("dp", "tensor"),
        P("dp", "tensor"),
        P("tensor", "dp"),
        P("dp"),
        P("dp"),
        P("dp", "tensor"),
        P("tensor", "dp"),
    )
    return jax.shard_map(body, mesh=mesh, in_specs=in_specs, out_specs=out_specs, check_vma=False)
```

profile of v0, /device:TPU:16, one launch (start us, length us, event | category | flops | bytes accessed | tf_op | source)
XLA Modules:
  0.0 1264.5 jit_solution(8206237857388793950)
XLA Ops:
  7.5 2.0 convert_reduce_fusion
  12.1 1.4 convolution_convert_fusion.7
  14.8 3.1 convolution_convert_fusion.8
  17.8 2.9 convolution_convert_fusion.9
  20.8 2.0 copy.69
  22.7 2.0 copy.70
  24.7 3.3 fusion
  28.1 2.6 exponential_reduce_fusion
  30.7 1.7 copy-done.2
  32.5 3.4 convolution_convert_fusion.2
  36.6 2.6 fusion.73
  40.3 1.4 convolution_convert_fusion.10
  41.7 2.1 convolution_convert_fusion.11
  43.7 69.4 %all-reduce.14.cloned.1.call-done = f32[832,1024]{1,0:T(8,128)} async-done(((f32[832,1024]{1,0:T(8,128)}), f32[832,1024]{1,0:T(8,128)}) %all-reduce.14.cloned.1.call-update) | async-done | bytes 3407888 | tf_op jit(solution)/shard_map/psum | solution.py:139
  113.2 2.9 fusion.71
  120.4 2.0 copy.73
  122.4 1.9 fusion.36
  127.4 2.4 fusion.74
  129.9 72.9 %all-reduce.16.cloned.1.call-done = f32[832,1024]{1,0:T(8,128)} async-done(((f32[832,1024]{1,0:T(8,128)}), f32[832,1024]{1,0:T(8,128)}) %all-reduce.16.cloned.1.call-update) | async-done | bytes 3407888 | tf_op jit(solution)/shard_map/psum | solution.py:150
  202.8 3.4 fusion.70
  207.0 10.6 multiply_convert_fusion.2
  217.6 2.9 fusion.24
  221.6 3.7 fusion.76
  225.8 72.5 %all-reduce.18.cloned.1.call-done = f32[832,1024]{1,0:T(8,128)} async-done(((f32[832,1024]{1,0:T(8,128)}), f32[832,1024]{1,0:T(8,128)}) %all-reduce.18.cloned.1.call-update) | async-done | bytes 3407888 | tf_op jit(solution)/shard_map/psum | solution.py:167
  298.4 4.5 multiply_reduce_fusion.1
  302.9 2.8 multiply_add_fusion.1
  305.7 1.8 copy-done.13
  308.5 3.2 multiply_reduce_fusion.4
  314.3 2.4 fusion.77
  316.9 2.9 convolution_convert_fusion.12
  321.2 6.5 fusion.75
  331.4 58.4 %all-reduce.20.cloned.1.call-done = f32[832,1024]{1,0:T(8,128)} async-done(((f32[832,1024]{1,0:T(8,128)}), f32[832,1024]{1,0:T(8,128)}) %all-reduce.20.cloned.1.call-update) | async-done | bytes 3407888 | tf_op jit(solution)/shard_map/psum | solution.py:186
  389.8 4.5 multiply_reduce_fusion.2
  394.3 3.8 multiply_add_fusion
  398.1 1.7 copy-done.11
  400.9 10.9 multiply_reduce_fusion
  411.8 6.7 multiply_convert_fusion
  418.5 1.9 fusion.47
  423.6 3.1 convolution_convert_fusion.1
  426.7 2.4 add_add_fusion
  429.5 4.0 fusion.52
  433.5 1.8 fusion.84
  435.4 3.9 fusion.49
  441.4 2.8 fusion.83
  444.3 3.3 fusion.81
  447.6 3.2 fusion.82
  450.9 7.1 fusion.67
  458.1 6.3 fusion.41
  466.3 1.7 copy.80
  468.0 54.7 %reduce-scatter.21.cloned.1.call-done = f32[128,256]{0,1:T(8,128)} async-done(((f32[1024,256]{0,1:T(8,128)}), f32[128,256]{0,1:T(8,128)}) %reduce-scatter.21.cloned.1.call-update) | async-done | bytes 131088 | tf_op jit(solution)/shard_map/reduce_scatter | solution.py:243
  522.6 1.7 copy.79
  524.3 147.0 %all-reduce.22.cloned.1.call-done = (f32[832,1024]{1,0:T(8,128)}, f32[832,1024]{1,0:T(8,128)}, f32[1,256,1024]{2,1,0:T(8,128)}) async-done(((f32[832,1024]{1,0:T(8,128)}, f32[832,1024]{1,0:T(8,128)}, f32[1,256,1024]{2,1,0:T(8,128)}), (f32[832,1024]{1,0:T(8,128)}, f32[832,1024]{1,0:T(8,128)}, f32[1,256,1024]{2,1,0:T(8,128)})) %all-reduce.22.cloned.1.call-update) | async-done | bytes 7864336 | tf_op jit(solution)/shard_map/psum | solution.py:158
  671.2 3.4 fusion.17
  674.6 31.9 %all-reduce.6 = (f32[1024]{0:T(1024)S(1)}, f32[1024]{0:T(1024)S(1)}, f32[1024]{0:T(1024)S(1)}, f32[1024]{0:T(1024)S(1)}, f32[1024]{0:T(1024)S(1)}, /*index=5*/f32[1024]{0:T(1024)S(1)}) all-reduce(f32[1024]{0:T(1024)S(1)} %get-tuple-element.80, f32[1024]{0:T(1024)S(1)} %get-tuple-element.87, ...), channel_id=2, replica_groups=mesh['dp'=8,'tensor'=4] {'dp'}, use_global_device_ids=true, to_apply=%region_26.27.clone | all-reduce | flops 6144 | bytes 49152
  710.0 5.0 fusion.38
  716.2 2.2 fusion.40
  718.4 20.1 %reduce-scatter.25.cloned.1.call-done = f32[256,128]{1,0:T(8,128)} async-done(((f32[256,1024]{1,0:T(8,128)}), f32[256,128]{1,0:T(8,128)}) %reduce-scatter.25.cloned.1.call-update) | async-done | bytes 131088 | tf_op jit(solution)/shard_map/reduce_scatter | solution.py:245
  738.5 67.0 %reduce-scatter.19.cloned.1.call-done = f32[128,256]{1,0:T(8,128)} async-done(((f32[1024,256]{1,0:T(8,128)}), f32[128,256]{1,0:T(8,128)}) %reduce-scatter.19.cloned.1.call-update) | async-done | bytes 131088 | tf_op jit(solution)/shard_map/reduce_scatter | solution.py:242
  805.5 66.7 %reduce-scatter.17.cloned.1.call-done = f32[256,128]{1,0:T(8,128)} async-done(((f32[256,1024]{1,0:T(8,128)}), f32[256,128]{1,0:T(8,128)}) %reduce-scatter.17.cloned.1.call-update) | async-done | bytes 131088 | tf_op jit(solution)/shard_map/reduce_scatter | solution.py:239
  872.2 66.9 %reduce-scatter.15.cloned.1.call-done = f32[128,256]{1,0:T(8,128)} async-done(((f32[1024,256]{1,0:T(8,128)}), f32[128,256]{1,0:T(8,128)}) %reduce-scatter.15.cloned.1.call-update) | async-done | bytes 131088 | tf_op jit(solution)/shard_map/reduce_scatter | solution.py:238
  939.1 66.2 %reduce-scatter.11.cloned.1.call-done = f32[128,256]{1,0:T(8,128)} async-done(((f32[1024,256]{1,0:T(8,128)}), f32[128,256]{1,0:T(8,128)}) %reduce-scatter.11.cloned.1.call-update) | async-done | bytes 131088 | tf_op jit(solution)/shard_map/reduce_scatter | solution.py:236
  1005.3 66.7 %reduce-scatter.13.cloned.1.call-done = f32[128,256]{1,0:T(8,128)} async-done(((f32[1024,256]{1,0:T(8,128)}), f32[128,256]{1,0:T(8,128)}) %reduce-scatter.13.cloned.1.call-update) | async-done | bytes 131088 | tf_op jit(solution)/shard_map/reduce_scatter | solution.py:237
  1072.1 91.8 %reduce-scatter.27.cloned.1.call-done = f32[128,1024]{1,0:T(8,128)} async-done(((f32[1024,1024]{1,0:T(8,128)}), f32[128,1024]{1,0:T(8,128)}) %reduce-scatter.27.cloned.1.call-update) | async-done | bytes 524304 | tf_op jit(solution)/shard_map/reduce_scatter | solution.py:248
  1163.9 92.7 %reduce-scatter.29.cloned.1.call-done = f32[1024,128]{1,0:T(8,128)} async-done(((f32[1024,1024]{1,0:T(8,128)}), f32[1024,128]{1,0:T(8,128)}) %reduce-scatter.29.cloned.1.call-update) | async-done | bytes 524304 | tf_op jit(solution)/shard_map/reduce_scatter | solution.py:249
  (222 shorter events, 37.2 us)
Async XLA Ops:
  7.2 199.6 %copy-start = (bf16[1024,1024]{1,0:T(8,128)(2,1)S(1)}, bf16[1024,1024]{1,0:T(8,128)(2,1)}, u32[]{:S(2)}) copy-start(bf16[1024,1024]{1,0:T(8,128)(2,1)} %param.37) | copy-start | bytes 6291460
  7.2 3.0 copy-start.56
  7.2 3.0 copy-start.59
  7.2 105.9 %all-reduce.14.cloned.1.call-start = ((), (), s32[]{:S(2)}) async-start(), calls=%async_computation.10 | async-start | bytes 6815744 | tf_op jit(solution)/shard_map/psum | solution.py:139
  7.3 2.3 copy-start.5
  7.5 4.6 copy-start.49
  14.8 10.0 copy-start.25
  28.0 4.4 copy-start.2
  28.1 4.4 copy-start.37
  32.5 4.2 copy-start.34
  39.3 163.5 %all-reduce.16.cloned.1.call-start = ((), (), s32[]{:S(2)}) async-start(), calls=%async_computation.11 | async-start | bytes 6815744 | tf_op jit(solution)/shard_map/psum | solution.py:150
  40.3 85.2 %copy-start.62 = (pred[256]{0:T(512)(128)(4,1)}, pred[256]{0:T(512)(128)(4,1)S(1)}, u32[]{:S(2)}) copy-start(pred[256]{0:T(512)(128)(4,1)S(1)} %iota_compare_fusion.1) | copy-start | bytes 772
  116.6 2.4 copy-start.46
  122.4 3.2 copy-start.44
  124.2 2.4 copy-start.9
  124.2 3.1 copy-start.32
  129.8 168.5 %all-reduce.18.cloned.1.call-start = ((), (), s32[]{:S(2)}) async-start(), calls=%async_computation.12 | async-start | bytes 6815744 | tf_op jit(solution)/shard_map/psum | solution.py:167
  206.2 11.3 copy-start.4
  207.0 10.6 copy-start.40
  207.0 10.6 copy-start.65
  225.4 77.5 %copy-start.41 = (bf16[1,832,1024]{2,1,0:T(8,128)(2,1)S(1)}, bf16[1,832,1024]{2,1,0:T(8,128)(2,1)}, u32[]{:S(2)}) copy-start(bf16[1,832,1024]{2,1,0:T(8,128)(2,1)} %param.39) | copy-start | bytes 5111812
  225.4 164.4 %all-reduce.20.cloned.1.call-start = ((), (), s32[]{:S(2)}) async-start(), calls=%async_computation.13 | async-start | bytes 6815744 | tf_op jit(solution)/shard_map/psum | solution.py:186
  298.3 4.5 copy-start.15
  302.9 4.6 copy-start.33
  308.4 3.3 copy-start.39
  308.5 3.3 copy-start.10
  311.7 2.6 copy-start.47
  316.8 149.5 %reduce-scatter.23.cloned.1.call-start = ((), (), s32[]{:S(2)}) async-start(), calls=%async_computation.20 | async-start | bytes 1179648 | tf_op jit(solution)/shard_map/reduce_scatter | solution.py:244
  321.1 201.5 %reduce-scatter.21.cloned.1.call-start = ((), (), s32[]{:S(2)}) async-start(), calls=%async_computation.19 | async-start | bytes 1179648 | tf_op jit(solution)/shard_map/reduce_scatter | solution.py:243
  321.2 6.5 copy-start.24
  321.2 7.0 copy-start.30
  331.4 339.9 %all-reduce.22.cloned.1.call-start = ((), (), s32[]{:S(2)}) async-start(), calls=%async_computation.24 | async-start | bytes 15728640 | tf_op jit(solution)/shard_map/psum | solution.py:158
  389.8 4.5 copy-start.14
  394.3 5.6 copy-start.35
  400.8 11.0 slice-start
  400.9 10.9 slice-start.1
  400.9 10.9 slice-start.2
  411.8 6.7 copy-start.27
  418.5 1.9 copy-start.26
  421.6 2.0 copy-start.22
  423.6 3.1 copy-start.51
  426.7 2.5 copy-start.36
  429.2 4.3 copy-start.18
  429.2 4.3 copy-start.21
  429.2 309.3 %reduce-scatter.25.cloned.1.call-start = ((), (), s32[]{:S(2)}) async-start(), calls=%async_computation.21 | async-start | bytes 1179648 | tf_op jit(solution)/shard_map/reduce_scatter | solution.py:245
  433.5 372.0 %reduce-scatter.19.cloned.1.call-start = ((), (), s32[]{:S(2)}) async-start(), calls=%async_computation.18 | async-start | bytes 1179648 | tf_op jit(solution)/shard_map/reduce_scatter | solution.py:242
  435.3 4.1 copy-start.6
  435.3 4.1 copy-start.53
  435.3 4.1 copy-start.55
  435.3 4.1 copy-start.57
  435.3 4.1 copy-start.60
  435.4 436.8 %reduce-scatter.17.cloned.1.call-start = ((), (), s32[]{:S(2)}) async-start(), calls=%async_computation.17 | async-start | bytes 1179648 | tf_op jit(solution)/shard_map/reduce_scatter | solution.py:239
  439.4 499.7 %reduce-scatter.15.cloned.1.call-start = ((), (), s32[]{:S(2)}) async-start(), calls=%async_computation.16 | async-start | bytes 1179648 | tf_op jit(solution)/shard_map/reduce_scatter | solution.py:238
  441.4 2.9 copy-start.23
  444.2 561.1 %reduce-scatter.11.cloned.1.call-start = ((), (), s32[]{:S(2)}) async-start(), calls=%async_computation.14 | async-start | bytes 1179648 | tf_op jit(solution)/shard_map/reduce_scatter | solution.py:236
  447.5 3.4 copy-start.67
  447.6 624.5 %reduce-scatter.13.cloned.1.call-start = ((), (), s32[]{:S(2)}) async-start(), calls=%async_computation.15 | async-start | bytes 1179648 | tf_op jit(solution)/shard_map/reduce_scatter | solution.py:237
  450.9 713.1 %reduce-scatter.27.cloned.1.call-start = ((), (), s32[]{:S(2)}) async-start(), calls=%async_computation.22 | async-start | bytes 4718592 | tf_op jit(solution)/shard_map/reduce_scatter | solution.py:248
  458.0 798.6 %reduce-scatter.29.cloned.1.call-start = ((), (), s32[]{:S(2)}) async-start(), calls=%async_computation.23 | async-start | bytes 4718592 | tf_op jit(solution)/shard_map/reduce_scatter | solution.py:249
  710.0 5.0 copy-start.7
  710.0 5.0 copy-start.12
  710.0 6.2 copy-start.16
  716.2 540.5 %copy-start.43 = (f32[1,256,1024]{2,1,0:T(8,128)S(1)}, f32[1,256,1024]{2,1,0:T(8,128)}, u32[]{:S(2)}) copy-start(f32[1,256,1024]{2,1,0:T(8,128)} %get-tuple-element.116) | copy-start | bytes 3145732
  716.2 541.4 %copy-start.1 = (bf16[1024,1024]{1,0:T(8,128)(2,1)S(1)}, bf16[1024,1024]{1,0:T(8,128)(2,1)}, u32[]{:S(2)}) copy-start(bf16[1024,1024]{1,0:T(8,128)(2,1)} %param.37) | copy-start | bytes 6291460
  (24 other events, 25.4 us)
Sparse Core Ops, SparseCore 0:
  39.4 73.7 all-reduce.13
  129.9 72.8 all-reduce.15
  225.5 72.8 all-reduce.17
  316.9 72.7 all-reduce.19
  393.0 63.0 reduce-scatter.22
  459.7 62.8 reduce-scatter.20
  525.7 145.4 all-reduce.21
  675.2 63.2 reduce-scatter.24
  742.9 62.5 reduce-scatter.18
  809.3 62.8 reduce-scatter.16
  876.6 62.5 reduce-scatter.14
  942.9 62.3 reduce-scatter.10
  1009.7 62.3 reduce-scatter.12
  1076.1 87.7 reduce-scatter.26
  1168.4 88.2 reduce-scatter.28
where the time goes:
time: 1280 us; the launch traced here: 1260 us
  waiting for transfers between devices  1010 us (79%)
  matrix products  119 us (9%)
  other arithmetic  50.1 us (4%)
  local copies, waits for them, and re-layouts  32.4 us (3%)
  blocking collectives  31.9 us (2%)
  between operations  16.7 us (1%)
    psum x1, waiting for transfers between devices, body(): lax.psum(jnp.dot(active_low, ffn_down, preferred_element_type=jnp.float32...  147 us
    reduce_scatter x1, waiting for transfers between devices, body(): lax.psum_scatter(down_grad, 'dp', scatter_dimension=1, tiled=True)  92.7 us
    reduce_scatter x1, waiting for transfers between devices, body(): lax.psum_scatter(up_grad, 'dp', scatter_dimension=0, tiled=True)  91.8 us
    psum x1, waiting for transfers between devices, body(): lax.psum(jnp.dot(mixed_two_rows, cross_o, preferred_element_type=jnp.floa...  72.9 us
    psum x1, waiting for transfers between devices, body(): norm_three_grad = lax.psum(against(inner_grad, ffn_up), 'tensor')  72.5 us
    psum x1, waiting for transfers between devices, body(): lax.psum(jnp.dot(mixed_one_rows, self_o, preferred_element_type=jnp.float...  69.4 us
    reduce_scatter x1, waiting for transfers between devices, body(): lax.psum_scatter(cq_grad, 'dp', scatter_dimension=0, tiled=True)  67 us
    reduce_scatter x1, waiting for transfers between devices, body(): lax.psum_scatter(sv_grad, 'dp', scatter_dimension=0, tiled=True)  66.9 us
  transfers between devices with their start and end apart: 15, of which 14 were waited for; matrix products, arithmetic and copies ran while one was open for 8% of the time, Pallas kernels for 0%

commit v1 on v0

--- a/solution.py
+++ b/solution.py
@@ -91,6 +91,44 @@
         key_grad.astype(jnp.bfloat16),
         value_grad.astype(jnp.bfloat16),
     )
+
+
+FLIPS = {"y": 1, "a": 2, "b": 6}
+
+
+def swap(value, axis, size, flip):
+    return lax.ppermute(value, axis, [(i, i ^ flip) for i in range(size)])
+
+
+def tensor_sum(value):
+    half = value.shape[0] // 2
+    core = lax.axis_index("tensor") & 1
+    keep = lax.dynamic_slice_in_dim(value, core * half, half)
+    send = lax.dynamic_slice_in_dim(value, (1 - core) * half, half)
+    mine = keep + swap(send, "tensor", 4, 1)
+    mine = mine + swap(mine, "tensor", 4, 2)
+    other = swap(mine, "tensor", 4, 1)
+    both = jnp.concatenate([mine, other, mine])
+    return lax.dynamic_slice_in_dim(both, core * half, 2 * half)
+
+
+def scatter_sum(value, dp_size, order):
+    if dp_size != 8:
+        return lax.psum_scatter(value, "dp", scatter_dimension=0, tiled=True)
+    rows = value.shape[0] // 8
+    me = lax.axis_index("dp")
+    parts = [
+        lax.dynamic_slice_in_dim(value, (me ^ m) * rows, rows) for m in (0, 1, 2, 3, 6, 7, 4, 5)
+    ]
+    left = jnp.stack(parts).reshape(2, 2, 2, rows, value.shape[1])
+    axes = ["b", "a", "y"]
+    for name in order:
+        at = axes.index(name)
+        axes.pop(at)
+        keep = lax.index_in_dim(left, 0, at, keepdims=False)
+        send = lax.index_in_dim(left, 1, at, keepdims=False)
+        left = keep + swap(send, "dp", 8, FLIPS[name])
+    return left
 
 
 def gelu_exact(values):
@@ -136,9 +174,7 @@
     value_one = split_heads(project(norm_one_low, self_v), clip_count)
     mixed_one, total_one = attend_forward(query_one, key_one, value_one, causal)
     mixed_one_rows = mixed_one.reshape(row_count, -1)
-    first_sum = resid_in + lax.psum(
-        jnp.dot(mixed_one_rows, self_o, preferred_element_type=jnp.float32), "tensor"
-    )
+    first_sum = resid_in + tensor_sum(jnp.dot(mixed_one_rows, self_o, preferred_element_type=jnp.float32))
     norm_two, scaled_two, inverse_two = norm_forward(first_sum, ln2_gain, ln2_bias)
     norm_two_low = norm_two.astype(jnp.bfloat16)
     text_flat = text_states.reshape(clip_count * text_rows, model_width)
@@ -147,30 +183,26 @@
     value_two = split_heads(project(text_flat, cross_v), clip_count)
     mixed_two, total_two = attend_forward(query_two, key_two, value_two, text_mask)
     mixed_two_rows = mixed_two.reshape(row_count, -1)
-    second_sum = first_sum + lax.psum(
-        jnp.dot(mixed_two_rows, cross_o, preferred_element_type=jnp.float32), "tensor"
-    )
+    second_sum = first_sum + tensor_sum(jnp.dot(mixed_two_rows, cross_o, preferred_element_type=jnp.float32))
     norm_three, scaled_three, inverse_three = norm_forward(second_sum, ln3_gain, ln3_bias)
     norm_three_low = norm_three.astype(jnp.bfloat16)
     inner_pre = jnp.dot(norm_three_low, ffn_up, preferred_element_type=jnp.float32)
     active, gelu_pull = jax.vjp(gelu_exact, inner_pre)
     active_low = active.astype(jnp.bfloat16)
-    final_sum = second_sum + lax.psum(
-        jnp.dot(active_low, ffn_down, preferred_element_type=jnp.float32), "tensor"
-    )
+    final_sum = second_sum + tensor_sum(jnp.dot(active_low, ffn_down, preferred_element_type=jnp.float32))
     output = final_sum.astype(jnp.bfloat16).reshape(clip_count, frames, model_width)
     out_grad = cotangent.reshape(row_count, model_width)
-    down_grad = over_rows(active_low, out_grad)
+    down_grad = over_rows(out_grad, active_low)
     active_grad = against(out_grad, ffn_down).astype(jnp.bfloat16)
     inner_grad = gelu_pull(active_grad.astype(jnp.float32))[0].astype(jnp.bfloat16)
     up_grad = over_rows(norm_three_low, inner_grad)
-    norm_three_grad = lax.psum(against(inner_grad, ffn_up), "tensor")
+    norm_three_grad = tensor_sum(against(inner_grad, ffn_up))
     delta_in, gain3_grad, bias3_grad = norm_backward(
         norm_three_grad, scaled_three, inverse_three, ln3_gain
     )
     grad_resid = out_grad.astype(jnp.float32) + delta_in
     resid_low = grad_resid.astype(jnp.bfloat16)
-    co_grad = over_rows(mixed_two_rows, resid_low)
+    co_grad = over_rows(resid_low, mixed_two_rows)
     mixed_two_grad = split_heads(against(resid_low, cross_o).astype(jnp.bfloat16), clip_count)
     query_two_grad, key_two_grad, value_two_grad = attend_backward(
         query_two, key_two, value_two, text_mask, total_two, mixed_two_grad
@@ -183,14 +215,14 @@
     cv_grad = over_rows(text_flat, value_two_rows)
     norm_two_part = against(query_two_rows, cross_q)
     text_part = against(key_two_rows, cross_k) + against(value_two_rows, cross_v)
-    norm_two_grad, text_sum = lax.psum((norm_two_part, text_part), "tensor")
+    norm_two_grad, text_sum = (tensor_sum(norm_two_part), tensor_sum(text_part))
     text_grad = text_sum.reshape(clip_count, text_rows, model_width)
     delta_in, gain2_grad, bias2_grad = norm_backward(
         norm_two_grad, scaled_two, inverse_two, ln2_gain
     )
     grad_resid = grad_resid + delta_in
     resid_low = grad_resid.astype(jnp.bfloat16)
-    so_grad = over_rows(mixed_one_rows, resid_low)
+    so_grad = over_rows(resid_low, mixed_one_rows)
     mixed_one_grad = split_heads(against(resid_low, self_o).astype(jnp.bfloat16), clip_count)
     query_one_grad, key_one_grad, value_one_grad = attend_backward(
         query_one, key_one, value_one, causal, total_one, mixed_one_grad
@@ -206,47 +238,31 @@
         + against(key_one_rows, self_k)
         + against(value_one_rows, self_v)
     )
-    norm_one_grad = lax.psum(norm_one_part, "tensor")
+    norm_one_grad = tensor_sum(norm_one_part)
     delta_in, gain1_grad, bias1_grad = norm_backward(
         norm_one_grad, scaled_one, inverse_one, ln1_gain
     )
     hidden_grad = (
         (grad_resid + delta_in).astype(jnp.bfloat16).reshape(clip_count, frames, model_width)
     )
-    (
-        gain1_grad,
-        bias1_grad,
-        sq_grad,
-        sk_grad,
-        sv_grad,
-        so_grad,
-        gain2_grad,
-        bias2_grad,
-        cq_grad,
-        ck_grad,
-        cv_grad,
-        co_grad,
-        gain3_grad,
-        bias3_grad,
-        up_grad,
-        down_grad,
-    ) = (
-        lax.psum_scatter(gain1_grad, "dp", scatter_dimension=0, tiled=True),
-        lax.psum_scatter(bias1_grad, "dp", scatter_dimension=0, tiled=True),
-        lax.psum_scatter(sq_grad, "dp", scatter_dimension=0, tiled=True),
-        lax.psum_scatter(sk_grad, "dp", scatter_dimension=0, tiled=True),
-        lax.psum_scatter(sv_grad, "dp", scatter_dimension=0, tiled=True),
-        lax.psum_scatter(so_grad, "dp", scatter_dimension=1, tiled=True),
-        lax.psum_scatter(gain2_grad, "dp", scatter_dimension=0, tiled=True),
-        lax.psum_scatter(bias2_grad, "dp", scatter_dimension=0, tiled=True),
-        lax.psum_scatter(cq_grad, "dp", scatter_dimension=0, tiled=True),
-        lax.psum_scatter(ck_grad, "dp", scatter_dimension=0, tiled=True),
-        lax.psum_scatter(cv_grad, "dp", scatter_dimension=0, tiled=True),
-        lax.psum_scatter(co_grad, "dp", scatter_dimension=1, tiled=True),
-        lax.psum_scatter(gain3_grad, "dp", scatter_dimension=0, tiled=True),
-        lax.psum_scatter(bias3_grad, "dp", scatter_dimension=0, tiled=True),
-        lax.psum_scatter(up_grad, "dp", scatter_dimension=0, tiled=True),
-        lax.psum_scatter(down_grad, "dp", scatter_dimension=1, tiled=True),
+    dp_size = lax.axis_size("dp")
+    up_grad = scatter_sum(up_grad, dp_size, "yab")
+    down_grad = scatter_sum(down_grad, dp_size, "aby").T
+    cross = scatter_sum(
+        jnp.concatenate([co_grad, cq_grad, ck_grad, cv_grad], 1), dp_size, "bya"
+    )
+    attn = scatter_sum(jnp.concatenate([sq_grad, sk_grad, so_grad], 1), dp_size, "yab")
+    vectors = jnp.stack(
+        [gain1_grad, bias1_grad, gain2_grad, bias2_grad, gain3_grad, bias3_grad] * 1, 1
+    )
+    last = scatter_sum(jnp.concatenate([sv_grad, jnp.pad(vectors, ((0, 0), (0, 122)))], 1), dp_size, "aby")
+    width = sq_grad.shape[1]
+    co_grad, cq_grad, ck_grad, cv_grad = (cross[:, i * width : (i + 1) * width] for i in range(4))
+    sq_grad, sk_grad, so_grad = (attn[:, i * width : (i + 1) * width] for i in range(3))
+    sv_grad = last[:, :width]
+    co_grad, so_grad = co_grad.T, so_grad.T
+    gain1_grad, bias1_grad, gain2_grad, bias2_grad, gain3_grad, bias3_grad = (
+        last[:, width + i] for i in range(6)
     )
     return (
         output,

time: 1280 us -> 606 us (0.47)
  waiting for transfers between devices: 1010 us -> 278 us
  local copies, waits for them, and re-layouts: 32.4 us -> 98.3 us
  other arithmetic: 50.1 us -> 95.9 us
  blocking collectives: 31.9 us -> 0 us
  matrix products: 119 us -> 92 us
  starting transfers between devices: 1.24 us -> 27.7 us
  between operations: 16.7 us -> 3.78 us
    reduce_scatter x10 -> x0, waiting for transfers between devices: 593 us -> none  [the longest x1 92.7 us: body(): lax.psum_scatter(down_grad, 'dp', scatter_dimension=1, tiled=True)]
    psum x5 -> x0, waiting for transfers between devices: 420 us -> none  [the longest x1 147 us: body(): lax.psum(jnp.dot(active_low, ffn_down, preferred_element_type=jnp.float32...]
    ppermute x0 -> x36, waiting for transfers between devices: none -> 278 us  [swap(): return lax.ppermute(value, axis, [(i, i ^ flip) for i in range(size)])]
    dynamic_slice x0 -> x34, local copies, waits for them, and re-layouts: none -> 38.8 us  [the longest x27 32.2 us: scatter_sum(): lax.dynamic_slice_in_dim(value, (me ^ m) * rows, rows)]
    add x0 -> x28, other arithmetic: none -> 38.4 us  [the longest x14 16.3 us: scatter_sum(): left = keep + swap(send, 'dp', 8, FLIPS[name])]
    unnamed x1 -> x0, blocking collectives: 31.9 us -> none
    ppermute x0 -> x36, starting transfers between devices: none -> 27.7 us  [swap(): return lax.ppermute(value, axis, [(i, i ^ flip) for i in range(size)])]
    dot_general x10, matrix products: 34.9 us -> 13.9 us  [over_rows(): lax.dot_general(left_op, right_op, (((0,), (0,)), ((), ())), preferred_el...]
  transfers between devices with their start and end apart: 15 -> 36, of which waited for: 14 -> 16; matrix products, arithmetic and copies ran while one was open for 8% -> 33% of each run, Pallas kernels for 0% -> 0%
where the time goes in v1:
time: 606 us; the launch traced here: 596 us
  waiting for transfers between devices  278 us (46%)
  local copies, waits for them, and re-layouts  98.3 us (16%)
  other arithmetic  95.9 us (16%)
  matrix products  92 us (15%)
  starting transfers between devices  27.7 us (5%)
    ppermute x36, waiting for transfers between devices, swap(): return lax.ppermute(value, axis, [(i, i ^ flip) for i in range(size)])  278 us
    unnamed x250, local copies, waits for them, and re-layouts  34.5 us
    dynamic_slice x27, local copies, waits for them, and re-layouts, scatter_sum(): lax.dynamic_slice_in_dim(value, (me ^ m) * rows, rows)  32.2 us
    ppermute x36, starting transfers between devices, swap(): return lax.ppermute(value, axis, [(i, i ^ flip) for i in range(size)])  27.7 us
    dot_general x10, matrix products, against(): lax.dot_general(left_op, right_op, (((1,), (1,)), ((), ())), preferred_el...  16.5 us
    add x14, other arithmetic, scatter_sum(): left = keep + swap(send, 'dp', 8, FLIPS[name])  16.3 us
    add x7, other arithmetic, tensor_sum(): mine = keep + swap(send, 'tensor', 4, 1)  14.6 us
    dot_general x10, matrix products, over_rows(): lax.dot_general(left_op, right_op, (((0,), (0,)), ((), ())), preferred_el...  13.9 us
  transfers between devices with their start and end apart: 36, of which 16 were waited for; matrix products, arithmetic and copies ran while one was open for 33% of the time, Pallas kernels for 0%

profile of v1, /device:TPU:16, one launch (start us, length us, event | category | flops | bytes accessed | tf_op | source)
XLA Modules:
  0.0 595.7 jit_solution(3172704459430914888)
XLA Ops:
  1.0 2.1 convert_reduce_fusion
  3.0 2.1 fusion.18
  9.6 3.1 convolution_convert_fusion.8
  12.7 2.9 convolution_convert_fusion.9
  15.6 2.0 copy.82
  17.6 2.0 copy.83
  19.6 3.3 fusion
  23.0 2.6 exponential_reduce_fusion
  27.3 7.7 %convolution_convert_fusion.2 = bf16[4,64,832]{2,1,0:T(8,128)(2,1)S(1)} fusion(bf16[832,4,64]{0,2,1:T(8,128)(2,1)S(1)} %bitcast.423, f32[4,832,832]{1,2,0:T(8,128)} %copy-done.2, f32[4,832]{1,0:T(4,128)S(1)} %log_add_fusion.1, pred[832,832]{0,1:T(8,128)(4,1)S(1)} %iota_compare_fusion), kind=kOutput, calls=%fused_computation.154 | convolution fusion | flops 365707264 | bytes 12633088 | tf_op jit(solution)/shard_map/chqk,ckhd->cqhd/dot_general | solution.py:63
  39.1 3.9 collective-permute-done
  43.1 2.3 dynamic-slice_add_fusion.5
  46.9 37.8 %collective-permute-done.1 = f32[416,1024]{1,0:T(8,128)S(1)} collective-permute-done((f32[416,1024]{1,0:T(8,128)S(1)}, f32[416,1024]{1,0:T(8,128)S(1)}, u32[]{:S(2)}, u32[]{:S(2)}) %collective-permute-start.1) | collective-permute-done | bytes 1703968 | tf_op jit(solution)/shard_map/ppermute | solution.py:100
  90.1 3.0 fusion.107
  102.9 3.5 collective-permute-done.3
  108.3 37.8 %collective-permute-done.4 = f32[416,1024]{1,0:T(8,128)S(1)} collective-permute-done((f32[416,1024]{1,0:T(8,128)S(1)}, f32[416,1024]{1,0:T(8,128)S(1)}, u32[]{:S(2)}, u32[]{:S(2)}) %collective-permute-start.4) | collective-permute-done | bytes 1703968 | tf_op jit(solution)/shard_map/ppermute | solution.py:100
  146.5 3.6 collective-permute-done.5
  151.8 8.8 %multiply_convert_fusion.2 = (bf16[832,1024]{1,0:T(8,128)(2,1)S(1)}, f32[832,1024]{1,0:T(8,128)S(1)}, f32[832,1024]{1,0:T(8,128)S(1)}) fusion(bf16[1024,1024]{1,0:T(8,128)(2,1)S(1)} %copy-done, f32[832,1024]{1,0:T(8,128)S(1)} %get-tuple-element.100, f32[1024]{0:T(1024)S(1)} %copy-done.102, f32[1024]{0:T(1024)S(1)} %copy-done.92, ...), kind=kOutput, calls=%fused_computation.85 | convolution fusion | flops 1804468224 | bytes 14039552 | tf_op jit(solution)/shard_map/dot_general | solution.py:189
  160.6 3.1 fusion.24
  163.8 2.0 fusion.112
  167.5 1.9 fusion.111
  172.5 2.5 dynamic-slice_add_fusion.2
  176.6 3.9 fusion.57
  188.2 26.9 %collective-permute-done.10 = f32[416,1024]{1,0:T(8,128)S(1)} collective-permute-done((f32[416,1024]{1,0:T(8,128)S(1)}, f32[416,1024]{1,0:T(8,128)S(1)}, u32[]{:S(2)}, u32[]{:S(2)}) %collective-permute-start.10) | collective-permute-done | bytes 1703968 | tf_op jit(solution)/shard_map/ppermute | solution.py:100
  215.6 3.2 fusion.99
  218.9 32.2 %collective-permute-done.7 = f32[416,1024]{1,0:T(8,128)S(1)} collective-permute-done((f32[416,1024]{1,0:T(8,128)S(1)}, f32[416,1024]{1,0:T(8,128)S(1)}, u32[]{:S(2)}, u32[]{:S(2)}) %collective-permute-start.7) | collective-permute-done | bytes 1703968 | tf_op jit(solution)/shard_map/ppermute | solution.py:100
  254.8 3.8 multiply_reduce_fusion.1
  258.6 3.0 multiply_add_fusion.1
  264.3 3.3 multiply_reduce_fusion.4
  273.0 2.0 fusion.52
  279.7 21.9 %collective-permute-done.30 = f32[2,2,128,1024]{3,2,1,0:T(8,128)} collective-permute-done((f32[2,2,128,1024]{3,2,1,0:T(8,128)}, f32[2,2,128,1024]{3,2,1,0:T(8,128)}, u32[]{:S(2)}, u32[]{:S(2)}) %collective-permute-start.30) | collective-permute-done | bytes 2097184 | tf_op jit(solution)/shard_map/ppermute | solution.py:100
  301.6 2.6 fusion.53
  306.9 18.5 %collective-permute-done.34 = f32[2,128,1024]{1,2,0:T(8,128)} collective-permute-done((f32[2,128,1024]{1,2,0:T(8,128)}, f32[2,128,1024]{1,2,0:T(8,128)}, u32[]{:S(2)}, u32[]{:S(2)}) %collective-permute-start.34) | collective-permute-done | bytes 1048608 | tf_op jit(solution)/shard_map/ppermute | solution.py:100
  326.9 2.2 dynamic-slice_add_fusion.1
  336.8 30.9 %collective-permute-done.13 = f32[416,1024]{1,0:T(8,128)S(1)} collective-permute-done((f32[416,1024]{1,0:T(8,128)S(1)}, f32[416,1024]{1,0:T(8,128)S(1)}, u32[]{:S(2)}, u32[]{:S(2)}) %collective-permute-start.13) | collective-permute-done | bytes 1703968 | tf_op jit(solution)/shard_map/ppermute | solution.py:100
  376.4 2.1 copy.117
  378.5 2.0 copy.116
  380.6 3.4 pad_maximum_fusion.3
  387.8 4.4 multiply_reduce_fusion.2
  398.0 7.8 %convolution_convert_fusion.1 = bf16[4,64,832]{2,1,0:T(8,128)(2,1)S(1)} fusion(bf16[832,4,64]{0,2,1:T(8,128)(2,1)} %bitcast.429, f32[4,832,832]{1,2,0:T(8,128)} %copy-done.2, f32[4,832]{1,0:T(4,128)S(1)} %copy-done.86, pred[832,832]{0,1:T(8,128)(4,1)S(1)} %copy-done.22), kind=kOutput, calls=%fused_computation.153 | convolution fusion | flops 365707264 | bytes 12633088 | tf_op jit(solution)/shard_map/chqk,cqhd->ckhd/dot_general | solution.py:72
  405.8 9.4 %multiply_reduce_fusion = (f32[4,832]{1,0:T(4,128)S(1)}, f32[4,832,832]{1,2,0:T(8,128)}) fusion(f32[4,832,832]{1,2,0:T(8,128)} %copy-done.2, f32[4,832]{1,0:T(4,128)S(1)} %copy-done.86, pred[832,832]{0,1:T(8,128)(4,1)S(1)} %copy-done.22, bf16[832,4,64]{0,2,1:T(8,128)(2,1)S(1)} %bitcast.430, bf16[832,4,64]{0,2,1:T(8,128)(2,1)S(1)} %bitcast.424), kind=kOutput, calls=%fused_computation.1 | convolution fusion | flops 368259840 | bytes 23721984 | tf_op jit(solution)/shard_map/cqhd,ckhd->chqk/dot_general | solution.py:78
  415.3 6.8 %multiply_convert_fusion = bf16[4,832,832]{1,2,0:T(8,128)(2,1)S(1)} fusion(f32[4,832,832]{1,2,0:T(8,128)} %get-tuple-element.144, f32[4,832,832]{1,2,0:T(8,128)S(1)} %bitcast.393, f32[4,832]{1,0:T(4,128)S(1)} %get-tuple-element.143, f32[4,832]{1,0:T(4,128)S(1)} %copy-done.86, pred[832,832]{0,1:T(8,128)(4,1)S(1)} %copy-done.22), kind=kLoop, calls=%fused_computation | loop fusion | flops 16613376 | bytes 28407808 | tf_op jit(solution)/shard_map/convert_element_type | solution.py:82
  425.2 2.4 fusion.114
  429.1 2.4 fusion.115
  434.9 1.9 copy.103
  436.8 1.9 copy.102
  438.7 1.9 copy.101
  442.4 3.9 add_add_fusion
  456.5 3.7 dynamic-slice_add_fusion
  461.0 2.7 slice_bitcast_fusion.4
  467.6 2.0 copy.114
  469.6 2.0 copy.113
  471.7 2.1 copy.112
  473.7 2.1 copy.111
  480.5 2.1 add.332
  485.0 6.5 %collective-permute-done.32 = f32[128,1024]{1,0:T(8,128)S(1)} collective-permute-done((f32[128,1024]{1,0:T(8,128)}, f32[128,1024]{1,0:T(8,128)S(1)}, u32[]{:S(2)}, u32[]{:S(2)}) %collective-permute-start.32) | collective-permute-done | bytes 524320 | tf_op jit(solution)/shard_map/ppermute | solution.py:100
  493.7 6.4 %collective-permute-done.16 = f32[416,1024]{1,0:T(8,128)} collective-permute-done((f32[416,1024]{1,0:T(8,128)}, f32[416,1024]{1,0:T(8,128)}, u32[]{:S(2)}, u32[]{:S(2)}) %collective-permute-start.16) | collective-permute-done | bytes 1703968 | tf_op jit(solution)/shard_map/ppermute | solution.py:100
  500.1 2.3 add.308
  502.5 2.1 fusion.61
  504.7 18.2 %collective-permute-done.28 = f32[2,128,1024]{2,1,0:T(8,128)S(1)} collective-permute-done((f32[2,128,1024]{2,1,0:T(8,128)S(1)}, f32[2,128,1024]{2,1,0:T(8,128)S(1)}, u32[]{:S(2)}, u32[]{:S(2)}) %collective-permute-start.28) | collective-permute-done | bytes 1048608 | tf_op jit(solution)/shard_map/ppermute | solution.py:100
  529.0 5.0 fusion.17
  548.0 3.0 collective-permute-start.21
  556.1 11.5 %collective-permute-done.21 = f32[2,2,128,384]{3,2,1,0:T(8,128)} collective-permute-done((f32[2,2,128,384]{3,2,1,0:T(8,128)S(1)}, f32[2,2,128,384]{3,2,1,0:T(8,128)}, u32[]{:S(2)}, u32[]{:S(2)}) %collective-permute-start.21) | collective-permute-done | bytes 786464 | tf_op jit(solution)/shard_map/ppermute | solution.py:100
  569.6 17.2 %collective-permute-done.22 = f32[2,128,384]{2,1,0:T(8,128)S(1)} collective-permute-done((f32[2,128,384]{2,1,0:T(8,128)S(1)}, f32[2,128,384]{2,1,0:T(8,128)S(1)}, u32[]{:S(2)}, u32[]{:S(2)}) %collective-permute-start.22) | collective-permute-done | bytes 393248 | tf_op jit(solution)/shard_map/ppermute | solution.py:100
  588.6 5.2 fusion.56
  (433 shorter events, 155.5 us)
Async XLA Ops:
  0.7 150.9 %copy-start = (bf16[1024,1024]{1,0:T(8,128)(2,1)S(1)}, bf16[1024,1024]{1,0:T(8,128)(2,1)}, u32[]{:S(2)}) copy-start(bf16[1024,1024]{1,0:T(8,128)(2,1)} %param.37) | copy-start | bytes 6291460
  0.9 26.4 %copy-start.21 = (pred[832,832]{0,1:T(8,128)(4,1)}, pred[832,832]{0,1:T(8,128)(4,1)S(1)}, u32[]{:S(2)}) copy-start(pred[832,832]{0,1:T(8,128)(4,1)S(1)} %iota_compare_fusion) | copy-start | bytes 2076676
  9.6 10.0 %copy-start.43 = (bf16[832,256]{0,1:T(8,128)(2,1)}, bf16[832,256]{0,1:T(8,128)(2,1)S(1)}, u32[]{:S(2)}) copy-start(bf16[832,256]{0,1:T(8,128)(2,1)S(1)} %copy.84) | copy-start | bytes 1277956
  39.1 3.9 collective-permute-start
  45.3 41.6 %copy-start.32 = (bf16[1,256,1024]{2,1,0:T(8,128)(2,1)S(1)}, bf16[1,256,1024]{2,1,0:T(8,128)(2,1)}, u32[]{:S(2)}) copy-start(bf16[1,256,1024]{2,1,0:T(8,128)(2,1)} %param.21) | copy-start | bytes 1572868
  45.3 41.6 %copy-start.55 = (bf16[1024,256]{1,0:T(8,128)(2,1)S(1)}, bf16[1024,256]{1,0:T(8,128)(2,1)}, u32[]{:S(2)}) copy-start(bf16[1024,256]{1,0:T(8,128)(2,1)} %param.32) | copy-start | bytes 1572868
  45.3 39.3 %collective-permute-start.1 = (f32[416,1024]{1,0:T(8,128)S(1)}, f32[416,1024]{1,0:T(8,128)S(1)}, u32[]{:S(2)}, u32[]{:S(2)}) collective-permute-start(f32[416,1024]{1,0:T(8,128)S(1)} %dynamic-slice_add_fusion.5), channel_id=1, source_target_pairs={{0,2},{1,3},{2,0},{3,1},{4,6},{5,7},{6,4},{7,5},{8,10},{9,11},{10,... | collective-permute-start | bytes 5111816 | tf_op jit(solution)/shard_map/ppermute | solution.py:100
  86.1 3.9 collective-permute-start.2
  87.0 180.7 %copy-start.98 = (pred[256]{0:T(512)(128)(4,1)}, pred[256]{0:T(512)(128)(4,1)S(1)}, u32[]{:S(2)}) copy-start(pred[256]{0:T(512)(128)(4,1)S(1)} %iota_compare_fusion.2) | copy-start | bytes 772
  87.3 11.2 %copy-start.76 = (bf16[256,256]{0,1:T(8,128)(2,1)}, bf16[256,256]{0,1:T(8,128)(2,1)S(1)}, u32[]{:S(2)}) copy-start(bf16[256,256]{0,1:T(8,128)(2,1)S(1)} %convolution_convert_fusion.10) | copy-start | bytes 393220
  100.7 167.0 %copy-start.83 = (f32[4,832]{1,0:T(4,128)}, f32[4,832]{1,0:T(4,128)S(1)}, u32[]{:S(2)}) copy-start(f32[4,832]{1,0:T(4,128)S(1)} %log_add_fusion) | copy-start | bytes 39940
  102.7 3.7 collective-permute-start.3
  106.7 43.4 %copy-start.4 = (f32[832,1024]{1,0:T(8,128)S(1)}, f32[832,1024]{1,0:T(8,128)}, u32[]{:S(2)}) copy-start(f32[832,1024]{1,0:T(8,128)} %copy-done.3) | copy-start | bytes 10223620
  106.7 39.3 %collective-permute-start.4 = (f32[416,1024]{1,0:T(8,128)S(1)}, f32[416,1024]{1,0:T(8,128)S(1)}, u32[]{:S(2)}, u32[]{:S(2)}) collective-permute-start(f32[416,1024]{1,0:T(8,128)S(1)} %dynamic-slice_add_fusion.4), channel_id=1, source_target_pairs={{0,2},{1,3},{2,0},{3,1},{4,6},{5,7},{6,4},{7,5},{8,10},{9,11},{10,... | collective-permute-start | bytes 5111816 | tf_op jit(solution)/shard_map/ppermute | solution.py:100
  146.4 3.7 collective-permute-start.5
  151.0 9.6 %copy-start.13 = (f32[832,1024]{1,0:T(8,128)}, f32[832,1024]{1,0:T(8,128)S(1)}, u32[]{:S(2)}) copy-start(f32[832,1024]{1,0:T(8,128)S(1)} %get-tuple-element.100) | copy-start | bytes 10223620
  151.7 8.9 %copy-start.101 = (bf16[1024,1024]{1,0:T(8,128)(2,1)S(1)}, bf16[1024,1024]{1,0:T(8,128)(2,1)}, u32[]{:S(2)}) copy-start(bf16[1024,1024]{1,0:T(8,128)(2,1)} %param.38) | copy-start | bytes 6291460
  165.9 6.7 %collective-permute-start.9 = (f32[416,1024]{1,0:T(8,128)S(1)}, f32[416,1024]{1,0:T(8,128)}, u32[]{:S(2)}, u32[]{:S(2)}) collective-permute-start(f32[416,1024]{1,0:T(8,128)S(1)} %constant_dynamic-slice_fusion.27), channel_id=1, source_target_pairs={{0,1},{1,0},{2,3},{3,2},{4,5},{5,4},{6,7},{7,6},{8,9},{9,8},{10,11... | collective-permute-start | bytes 5111816 | tf_op jit(solution)/shard_map/ppermute | solution.py:100
  172.4 8.5 %collective-permute-start.6 = (f32[416,1024]{1,0:T(8,128)}, f32[416,1024]{1,0:T(8,128)}, u32[]{:S(2)}, u32[]{:S(2)}) collective-permute-start(f32[416,1024]{1,0:T(8,128)} %constant_dynamic-slice_fusion.28), channel_id=1, source_target_pairs={{0,1},{1,0},{2,3},{3,2},{4,5},{5,4},{6,7},{7,6},{8,9},{9,8},{10,11... | collective-permute-start | bytes 5111816 | tf_op jit(solution)/shard_map/ppermute | solution.py:100
  175.0 40.1 %collective-permute-start.10 = (f32[416,1024]{1,0:T(8,128)S(1)}, f32[416,1024]{1,0:T(8,128)S(1)}, u32[]{:S(2)}, u32[]{:S(2)}) collective-permute-start(f32[416,1024]{1,0:T(8,128)S(1)} %dynamic-slice_add_fusion.2), channel_id=1, source_target_pairs={{0,2},{1,3},{2,0},{3,1},{4,6},{5,7},{6,4},{7,5},{8,10},{9,11},{10,... | collective-permute-start | bytes 5111816 | tf_op jit(solution)/shard_map/ppermute | solution.py:100
  184.2 66.9 %collective-permute-start.7 = (f32[416,1024]{1,0:T(8,128)S(1)}, f32[416,1024]{1,0:T(8,128)S(1)}, u32[]{:S(2)}, u32[]{:S(2)}) collective-permute-start(f32[416,1024]{1,0:T(8,128)S(1)} %dynamic-slice_add_fusion.3), channel_id=1, source_target_pairs={{0,2},{1,3},{2,0},{3,1},{4,6},{5,7},{6,4},{7,5},{8,10},{9,11},{10,... | collective-permute-start | bytes 5111816 | tf_op jit(solution)/shard_map/ppermute | solution.py:100
  185.1 30.4 %copy-start.35 = (f32[8,128,1024]{1,2,0:T(8,128)}, f32[8,128,1024]{1,2,0:T(8,128)S(1)}, u32[]{:S(2)}) copy-start(f32[8,128,1024]{1,2,0:T(8,128)S(1)} %bitcast_dynamic-update-slice_fusion) | copy-start | bytes 12582916
  186.6 28.9 %copy-start.14 = (f32[832,1024]{1,0:T(8,128)S(1)}, f32[832,1024]{1,0:T(8,128)}, u32[]{:S(2)}) copy-start(f32[832,1024]{1,0:T(8,128)} %copy-done.13) | copy-start | bytes 10223620
  186.7 28.9 %copy-start.106 = (bf16[832,1024]{1,0:T(8,128)(2,1)S(1)}, bf16[832,1024]{1,0:T(8,128)(2,1)}, u32[]{:S(2)}) copy-start(bf16[832,1024]{1,0:T(8,128)(2,1)} %copy-done.105) | copy-start | bytes 5111812
  186.7 86.1 %collective-permute-start.33 = (f32[2,2,128,1024]{2,3,1,0:T(8,128)}, f32[2,2,128,1024]{2,3,1,0:T(8,128)}, u32[]{:S(2)}, u32[]{:S(2)}) collective-permute-start(f32[2,2,128,1024]{2,3,1,0:T(8,128)} %slice_bitcast_fusion), channel_id=1, source_target_pairs={{0,8},{4,12},{8,0},{12,4},{16,24},{20,28},{24,16},{28,20},{1,9},{5... | collective-permute-start | bytes 6291464 | tf_op jit(solution)/shard_map/ppermute | solution.py:100
  215.5 39.3 %collective-permute-start.11 = (f32[416,1024]{1,0:T(8,128)S(1)}, f32[416,1024]{1,0:T(8,128)S(1)}, u32[]{:S(2)}, u32[]{:S(2)}) collective-permute-start(f32[416,1024]{1,0:T(8,128)S(1)} %add.300), channel_id=1, source_target_pairs={{0,1},{1,0},{2,3},{3,2},{4,5},{5,4},{6,7},{7,6},{8,9},{9,8},{10,11... | collective-permute-start | bytes 5111816 | tf_op jit(solution)/shard_map/ppermute | solution.py:100
  251.4 7.2 %collective-permute-start.8 = (f32[416,1024]{1,0:T(8,128)S(1)}, f32[416,1024]{1,0:T(8,128)S(1)}, u32[]{:S(2)}, u32[]{:S(2)}) collective-permute-start(f32[416,1024]{1,0:T(8,128)S(1)} %add.297), channel_id=1, source_target_pairs={{0,1},{1,0},{2,3},{3,2},{4,5},{5,4},{6,7},{7,6},{8,9},{9,8},{10,11... | collective-permute-start | bytes 5111816 | tf_op jit(solution)/shard_map/ppermute | solution.py:100
  253.3 48.3 %collective-permute-start.30 = (f32[2,2,128,1024]{3,2,1,0:T(8,128)}, f32[2,2,128,1024]{3,2,1,0:T(8,128)}, u32[]{:S(2)}, u32[]{:S(2)}) collective-permute-start(f32[2,2,128,1024]{3,2,1,0:T(8,128)} %slice_bitcast_fusion.2), channel_id=1, source_target_pairs={{0,4},{4,0},{8,12},{12,8},{16,20},{20,16},{24,28},{28,24},{1,5},{5... | collective-permute-start | bytes 6291464 | tf_op jit(solution)/shard_map/ppermute | solution.py:100
  272.6 54.3 %collective-permute-start.12 = (f32[416,1024]{1,0:T(8,128)}, f32[416,1024]{1,0:T(8,128)}, u32[]{:S(2)}, u32[]{:S(2)}) collective-permute-start(f32[416,1024]{1,0:T(8,128)} %constant_dynamic-slice_fusion.26), channel_id=1, source_target_pairs={{0,1},{1,0},{2,3},{3,2},{4,5},{5,4},{6,7},{7,6},{8,9},{9,8},{10,11... | collective-permute-start | bytes 5111816 | tf_op jit(solution)/shard_map/ppermute | solution.py:100
  277.4 48.0 %collective-permute-start.34 = (f32[2,128,1024]{1,2,0:T(8,128)}, f32[2,128,1024]{1,2,0:T(8,128)}, u32[]{:S(2)}, u32[]{:S(2)}) collective-permute-start(f32[2,128,1024]{1,2,0:T(8,128)} %slice_bitcast_fusion.6), channel_id=1, source_target_pairs={{0,24},{4,28},{8,16},{12,20},{16,8},{20,12},{24,0},{28,4},{1,25},{... | collective-permute-start | bytes 3145736 | tf_op jit(solution)/shard_map/ppermute | solution.py:100
  279.7 45.7 %copy-start.31 = (f32[2,2,128,1024]{2,3,1,0:T(8,128)S(1)}, f32[2,2,128,1024]{2,3,1,0:T(8,128)}, u32[]{:S(2)}) copy-start(f32[2,2,128,1024]{2,3,1,0:T(8,128)} %copy-done.30) | copy-start | bytes 6291460
  304.2 24.8 %copy-start.28 = (f32[2,2,128,1024]{3,2,1,0:T(8,128)}, f32[2,2,128,1024]{3,2,1,0:T(8,128)S(1)}, u32[]{:S(2)}) copy-start(f32[2,2,128,1024]{3,2,1,0:T(8,128)S(1)} %fusion.53) | copy-start | bytes 6291460
  304.3 22.6 %copy-start.26 = (f32[832,1024]{1,0:T(8,128)S(1)}, f32[832,1024]{1,0:T(8,128)}, u32[]{:S(2)}) copy-start(f32[832,1024]{1,0:T(8,128)} %copy-done.25) | copy-start | bytes 10223620
  305.3 158.4 %collective-permute-start.31 = (f32[2,128,1024]{2,1,0:T(8,128)}, f32[2,128,1024]{2,1,0:T(8,128)}, u32[]{:S(2)}, u32[]{:S(2)}) collective-permute-start(f32[2,128,1024]{2,1,0:T(8,128)} %slice_bitcast_fusion.8), channel_id=1, source_target_pairs={{0,8},{4,12},{8,0},{12,4},{16,24},{20,28},{24,16},{28,20},{1,9},{5... | collective-permute-start | bytes 3145736 | tf_op jit(solution)/shard_map/ppermute | solution.py:100
  329.1 38.5 %collective-permute-start.13 = (f32[416,1024]{1,0:T(8,128)S(1)}, f32[416,1024]{1,0:T(8,128)S(1)}, u32[]{:S(2)}, u32[]{:S(2)}) collective-permute-start(f32[416,1024]{1,0:T(8,128)S(1)} %dynamic-slice_add_fusion.1), channel_id=1, source_target_pairs={{0,2},{1,3},{2,0},{3,1},{4,6},{5,7},{6,4},{7,5},{8,10},{9,11},{10,... | collective-permute-start | bytes 5111816 | tf_op jit(solution)/shard_map/ppermute | solution.py:100
  331.5 151.2 %collective-permute-start.35 = (f32[128,1024]{0,1:T(8,128)}, f32[128,1024]{0,1:T(8,128)}, u32[]{:S(2)}, u32[]{:S(2)}) collective-permute-start(f32[128,1024]{0,1:T(8,128)} %slice_bitcast_fusion.16), channel_id=1, source_target_pairs={{0,4},{4,0},{8,12},{12,8},{16,20},{20,16},{24,28},{28,24},{1,5},{5... | collective-permute-start | bytes 1572872 | tf_op jit(solution)/shard_map/ppermute | solution.py:100
  336.3 48.1 %collective-permute-start.18 = (f32[128,1024]{1,0:T(8,128)}, f32[128,1024]{1,0:T(8,128)}, u32[]{:S(2)}, u32[]{:S(2)}) collective-permute-start(f32[128,1024]{1,0:T(8,128)} %constant_dynamic-slice_fusion.24), channel_id=1, source_target_pairs={{0,1},{1,0},{2,3},{3,2},{4,5},{5,4},{6,7},{7,6},{8,9},{9,8},{10,11... | collective-permute-start | bytes 1572872 | tf_op jit(solution)/shard_map/ppermute | solution.py:100
  336.7 32.7 %copy-start.34 = (bf16[832,1024]{1,0:T(8,128)(2,1)S(1)}, bf16[832,1024]{1,0:T(8,128)(2,1)}, u32[]{:S(2)}) copy-start(bf16[832,1024]{1,0:T(8,128)(2,1)} %copy-done.33) | copy-start | bytes 5111812
  369.1 18.7 %collective-permute-start.14 = (f32[416,1024]{1,0:T(8,128)}, f32[416,1024]{1,0:T(8,128)}, u32[]{:S(2)}, u32[]{:S(2)}) collective-permute-start(f32[416,1024]{1,0:T(8,128)} %add.303), channel_id=1, source_target_pairs={{0,1},{1,0},{2,3},{3,2},{4,5},{5,4},{6,7},{7,6},{8,9},{9,8},{10,11... | collective-permute-start | bytes 5111816 | tf_op jit(solution)/shard_map/ppermute | solution.py:100
  378.5 9.3 %copy-start.91 = (f32[1024]{0:T(1024)S(1)}, f32[1024]{0:T(1024)}, u32[]{:S(2)}) copy-start(f32[1024]{0:T(1024)} %param.29) | copy-start | bytes 12292
  383.9 96.5 %collective-permute-start.27 = (f32[2,2,128,1024]{3,2,1,0:T(8,128)}, f32[2,2,128,1024]{3,2,1,0:T(8,128)}, u32[]{:S(2)}, u32[]{:S(2)}) collective-permute-start(f32[2,2,128,1024]{3,2,1,0:T(8,128)} %bitcast.104), channel_id=1, source_target_pairs={{0,24},{4,28},{8,16},{12,20},{16,8},{20,12},{24,0},{28,4},{1,25},{... | collective-permute-start | bytes 6291464 | tf_op jit(solution)/shard_map/ppermute | solution.py:100
  386.3 91.2 %collective-permute-start.19 = (f32[128,1024]{1,0:T(8,128)}, f32[128,1024]{1,0:T(8,128)}, u32[]{:S(2)}, u32[]{:S(2)}) collective-permute-start(f32[128,1024]{1,0:T(8,128)} %dynamic-slice_add_fusion.6), channel_id=1, source_target_pairs={{0,2},{1,3},{2,0},{3,1},{4,6},{5,7},{6,4},{7,5},{8,10},{9,11},{10,... | collective-permute-start | bytes 1572872 | tf_op jit(solution)/shard_map/ppermute | solution.py:100
  398.0 17.3 %slice-start = ((s8[11927552]{0:T(1024)(128)(4,1)}), s8[4194304]{0:T(1024)(128)(4,1)S(1)}, s32[]{:S(2)}) async-start(s8[11927552]{0:T(1024)(128)(4,1)} %bitcast.392), calls=%async_computation | async-start | bytes 8388608
  398.0 17.3 %slice-start.1 = ((s8[11927552]{0:T(1024)(128)(4,1)}), s8[4194304]{0:T(1024)(128)(4,1)S(1)}, s32[]{:S(2)}) async-start(s8[11927552]{0:T(1024)(128)(4,1)} %bitcast.392), calls=%async_computation.1 | async-start | bytes 8388608
  405.8 36.6 %copy-start.64 = (bf16[4,64,832]{2,1,0:T(8,128)(2,1)}, bf16[4,64,832]{2,1,0:T(8,128)(2,1)S(1)}, u32[]{:S(2)}) copy-start(bf16[4,64,832]{2,1,0:T(8,128)(2,1)S(1)} %convolution_convert_fusion.1) | copy-start | bytes 1277956
  405.8 9.4 %slice-start.2 = ((s8[11927552]{0:T(1024)(128)(4,1)}), s8[3538944]{0:T(1024)(128)(4,1)S(1)}, s32[]{:S(2)}) async-start(s8[11927552]{0:T(1024)(128)(4,1)} %bitcast.392), calls=%async_computation.2 | async-start | bytes 7077888
  449.4 7.1 %collective-permute-start.15 = (f32[416,1024]{1,0:T(8,128)}, f32[416,1024]{1,0:T(8,128)}, u32[]{:S(2)}, u32[]{:S(2)}) collective-permute-start(f32[416,1024]{1,0:T(8,128)} %constant_dynamic-slice_fusion.25), channel_id=1, source_target_pairs={{0,1},{1,0},{2,3},{3,2},{4,5},{5,4},{6,7},{7,6},{8,9},{9,8},{10,11... | collective-permute-start | bytes 5111816 | tf_op jit(solution)/shard_map/ppermute | solution.py:100
  456.5 8.9 %copy-start.29 = (f32[2,2,128,1024]{3,2,1,0:T(8,128)S(1)}, f32[2,2,128,1024]{3,2,1,0:T(8,128)}, u32[]{:S(2)}) copy-start(f32[2,2,128,1024]{3,2,1,0:T(8,128)} %copy-done.28) | copy-start | bytes 6291460
  460.2 39.9 %collective-permute-start.16 = (f32[416,1024]{1,0:T(8,128)}, f32[416,1024]{1,0:T(8,128)}, u32[]{:S(2)}, u32[]{:S(2)}) collective-permute-start(f32[416,1024]{1,0:T(8,128)} %dynamic-slice_add_fusion), channel_id=1, source_target_pairs={{0,2},{1,3},{2,0},{3,1},{4,6},{5,7},{6,4},{7,5},{8,10},{9,11},{10,... | collective-permute-start | bytes 5111816 | tf_op jit(solution)/shard_map/ppermute | solution.py:100
  463.7 38.7 %collective-permute-start.24 = (f32[2,2,128,768]{3,2,1,0:T(8,128)}, f32[2,2,128,768]{3,2,1,0:T(8,128)}, u32[]{:S(2)}, u32[]{:S(2)}) collective-permute-start(f32[2,2,128,768]{3,2,1,0:T(8,128)} %slice_bitcast_fusion.4), channel_id=1, source_target_pairs={{0,4},{4,0},{8,12},{12,8},{16,20},{20,16},{24,28},{28,24},{1,5},{5... | collective-permute-start | bytes 4718600 | tf_op jit(solution)/shard_map/ppermute | solution.py:100
  477.5 14.1 %collective-permute-start.32 = (f32[128,1024]{1,0:T(8,128)}, f32[128,1024]{1,0:T(8,128)S(1)}, u32[]{:S(2)}, u32[]{:S(2)}) collective-permute-start(f32[128,1024]{1,0:T(8,128)} %slice_bitcast_fusion.18), channel_id=1, source_target_pairs={{0,24},{4,28},{8,16},{12,20},{16,8},{20,12},{24,0},{28,4},{1,25},{... | collective-permute-start | bytes 1572872 | tf_op jit(solution)/shard_map/ppermute | solution.py:100
  480.4 12.0 %collective-permute-start.20 = (f32[128,1024]{1,0:T(8,128)S(1)}, f32[128,1024]{1,0:T(8,128)S(1)}, u32[]{:S(2)}, u32[]{:S(2)}) collective-permute-start(f32[128,1024]{1,0:T(8,128)S(1)} %add.314), channel_id=1, source_target_pairs={{0,1},{1,0},{2,3},{3,2},{4,5},{5,4},{6,7},{7,6},{8,9},{9,8},{10,11... | collective-permute-start | bytes 1572872 | tf_op jit(solution)/shard_map/ppermute | solution.py:100
  482.7 40.3 %collective-permute-start.28 = (f32[2,128,1024]{2,1,0:T(8,128)S(1)}, f32[2,128,1024]{2,1,0:T(8,128)S(1)}, u32[]{:S(2)}, u32[]{:S(2)}) collective-permute-start(f32[2,128,1024]{2,1,0:T(8,128)S(1)} %slice_bitcast_fusion.10), channel_id=1, source_target_pairs={{0,4},{4,0},{8,12},{12,8},{16,20},{20,16},{24,28},{28,24},{1,5},{5... | collective-permute-start | bytes 3145736 | tf_op jit(solution)/shard_map/ppermute | solution.py:100
  502.4 26.6 %collective-permute-start.17 = (f32[416,1024]{1,0:T(8,128)S(1)}, f32[416,1024]{1,0:T(8,128)S(1)}, u32[]{:S(2)}, u32[]{:S(2)}) collective-permute-start(f32[416,1024]{1,0:T(8,128)S(1)} %add.308), channel_id=1, source_target_pairs={{0,1},{1,0},{2,3},{3,2},{4,5},{5,4},{6,7},{7,6},{8,9},{9,8},{10,11... | collective-permute-start | bytes 5111816 | tf_op jit(solution)/shard_map/ppermute | solution.py:100
  504.5 19.4 %copy-start.20 = (bf16[832,1024]{1,0:T(8,128)(2,1)S(1)}, bf16[832,1024]{1,0:T(8,128)(2,1)}, u32[]{:S(2)}) copy-start(bf16[832,1024]{1,0:T(8,128)(2,1)} %fusion.55) | copy-start | bytes 5111812
  504.5 19.4 %copy-start.65 = (bf16[4,64,832]{2,1,0:T(8,128)(2,1)S(1)}, bf16[4,64,832]{2,1,0:T(8,128)(2,1)}, u32[]{:S(2)}) copy-start(bf16[4,64,832]{2,1,0:T(8,128)(2,1)} %copy-done.64) | copy-start | bytes 1277956
  504.6 21.0 %collective-permute-start.25 = (f32[2,128,768]{2,1,0:T(8,128)S(1)}, f32[2,128,768]{2,1,0:T(8,128)S(1)}, u32[]{:S(2)}, u32[]{:S(2)}) collective-permute-start(f32[2,128,768]{2,1,0:T(8,128)S(1)} %slice_bitcast_fusion.12), channel_id=1, source_target_pairs={{0,8},{4,12},{8,0},{12,4},{16,24},{20,28},{24,16},{28,20},{1,9},{5... | collective-permute-start | bytes 2359304 | tf_op jit(solution)/shard_map/ppermute | solution.py:100
  523.9 27.1 %collective-permute-start.29 = (f32[128,1024]{1,0:T(8,128)}, f32[128,1024]{1,0:T(8,128)}, u32[]{:S(2)}, u32[]{:S(2)}) collective-permute-start(f32[128,1024]{1,0:T(8,128)} %slice_bitcast_fusion.20), channel_id=1, source_target_pairs={{0,8},{4,12},{8,0},{12,4},{16,24},{20,28},{24,16},{28,20},{1,9},{5... | collective-permute-start | bytes 1572872 | tf_op jit(solution)/shard_map/ppermute | solution.py:100
  527.4 26.2 %collective-permute-start.26 = (f32[128,768]{1,0:T(8,128)}, f32[128,768]{1,0:T(8,128)}, u32[]{:S(2)}, u32[]{:S(2)}) collective-permute-start(f32[128,768]{1,0:T(8,128)} %slice_bitcast_fusion.22), channel_id=1, source_target_pairs={{0,24},{4,28},{8,16},{12,20},{16,8},{20,12},{24,0},{28,4},{1,25},{... | collective-permute-start | bytes 1179656 | tf_op jit(solution)/shard_map/ppermute | solution.py:100
  543.2 10.4 %copy-start.54 = (f32[2,128,768]{2,1,0:T(8,128)S(1)}, f32[2,128,768]{2,1,0:T(8,128)}, u32[]{:S(2)}) copy-start(f32[2,128,768]{2,1,0:T(8,128)} %copy-done.53) | copy-start | bytes 2359300
  548.0 19.6 %collective-permute-start.21 = (f32[2,2,128,384]{3,2,1,0:T(8,128)S(1)}, f32[2,2,128,384]{3,2,1,0:T(8,128)}, u32[]{:S(2)}, u32[]{:S(2)}) collective-permute-start(f32[2,2,128,384]{3,2,1,0:T(8,128)S(1)} %slice_bitcast_fusion.14), channel_id=1, source_target_pairs={{0,8},{4,12},{8,0},{12,4},{16,24},{20,28},{24,16},{28,20},{1,9},{5... | collective-permute-start | bytes 2359304 | tf_op jit(solution)/shard_map/ppermute | solution.py:100
  552.1 17.5 %copy-start.97 = (f32[832]{0:T(1024)S(1)}, f32[832]{0:T(1024)}, u32[]{:S(2)}) copy-start(f32[832]{0:T(1024)} %get-tuple-element.81) | copy-start | bytes 9988
  569.1 17.7 %collective-permute-start.22 = (f32[2,128,384]{2,1,0:T(8,128)S(1)}, f32[2,128,384]{2,1,0:T(8,128)S(1)}, u32[]{:S(2)}, u32[]{:S(2)}) collective-permute-start(f32[2,128,384]{2,1,0:T(8,128)S(1)} %slice_bitcast_fusion.24), channel_id=1, source_target_pairs={{0,24},{4,28},{8,16},{12,20},{16,8},{20,12},{24,0},{28,4},{1,25},{... | collective-permute-start | bytes 1179656 | tf_op jit(solution)/shard_map/ppermute | solution.py:100
  586.9 6.9 %collective-permute-start.23 = (f32[128,384]{1,0:T(8,128)S(1)}, f32[128,384]{1,0:T(8,128)S(1)}, u32[]{:S(2)}, u32[]{:S(2)}) collective-permute-start(f32[128,384]{1,0:T(8,128)S(1)} %slice_bitcast_fusion.26), channel_id=1, source_target_pairs={{0,4},{4,0},{8,12},{12,8},{16,20},{20,16},{24,28},{28,24},{1,5},{5... | collective-permute-start | bytes 589832 | tf_op jit(solution)/shard_map/ppermute | solution.py:100
  (82 other events, 294.3 us)
